TPU v7x, 256 devices: a whole 4x4x8 slice. The times are simulated.
256 devices in a mesh: px: 16 (over y, x), py: 16 (over z, core).
Axes of the slice: x: 4, y: 4, z: 8, core: 2. Of those that a mesh axis runs over, the one named last changes fastest.
Arguments:
- start_field: float32 [128, 256, 512], P('px', 'py'), may hold values from -1.7 to 1.7
- known: float32 [8, 128, 256, 512], P(None, 'px', 'py'), may hold values from -1 to 1
Outputs:
- solution_field: float32 [128, 256, 512], P('px', 'py')
- residual: float32 [128, 256, 512], P('px', 'py')
All inputs are finite; a program needn't handle non-finite values.
Results may differ from a plain program's by a relative error of at most 0.01.
Values sent between devices are 32-bit elements; how exact they have to be, the bound alone decides.
No kernel may reach another device: no remote copies, remote signals or barrier semaphores. Data moves between devices by JAX's collectives and lax.ppermute only.
A program may use at most 64 MiB of HBM per device.

v0:
```python
import jax
import jax.numpy as jnp
from jax import lax
from jax.sharding import PartitionSpec as P

NEWTON = 2
ITERS = 3
DIFFUSION = 0.5
SHIFT = 4.0
EPS = 1e-06


def extended(cells, sides, width):
    for axis, dim in sides:
        count = lax.axis_size(axis)
        ends = count - 1
        head = lax.slice_in_dim(cells, 0, width, axis=dim)
        tail = lax.slice_in_dim(cells, cells.shape[dim] - width, cells.shape[dim], axis=dim)
        cells = jnp.concatenate(
            [
                lax.ppermute(tail, axis, [(i, (i + 1) % count) for i in range(ends)]),
                cells,
                lax.ppermute(head, axis, [((i + 1) % count, i) for i in range(ends)]),
            ],
            axis=dim,
        )
    return cells


def laplace(field):
    padded = extended(field, (("px", 0), ("py", 1)), 1)
    zero = jnp.zeros_like(field[:, :, :1])
    upper = jnp.concatenate([field[:, :, 1:], zero], axis=2)
    lower = jnp.concatenate([zero, field[:, :, :-1]], axis=2)
    beside = padded[2:, 1:-1, :] + padded[:-2, 1:-1, :]
    beside = beside + padded[1:-1, 2:, :] + padded[1:-1, :-2, :]
    return beside + upper + lower - 6.0 * field


def allen_cahn(field, lap):
    return DIFFUSION * lap + field - field * field * field


def solve_small(hess, beta):
    normal = jnp.sum(hess[:, :, None] * hess[:, None, :], axis=0)
    target = beta * hess[0]
    lower = jnp.linalg.cholesky(normal)
    count = normal.shape[0]
    forward = []
    for i in range(count):
        acc = target[i]
        for j in range(i):
            acc = acc - lower[i, j] * forward[j]
        forward.append(acc / lower[i, i])
    back = [None] * count
    for i in reversed(range(count)):
        acc = forward[i]
        for j in range(i + 1, count):
            acc = acc - lower[j, i] * back[j]
        back[i] = acc / lower[i, i]
    return jnp.stack(back)


def local(start_field, known):
    cells = float(
        start_field.shape[0]
        * lax.axis_size("px")
        * start_field.shape[1]
        * lax.axis_size("py")
        * start_field.shape[2]
    )
    field = start_field
    lap_field = laplace(field)
    for step in range(NEWTON):
        force = allen_cahn(field, lap_field)
        diffs = field[None] - known
        dist_local = jnp.sum(diffs * diffs, axis=(1, 2, 3))
        first_sum, force_sq = lax.psum((dist_local, jnp.sum(force * force)), ("px", "py"))
        beta = jnp.sqrt(force_sq + EPS)
        basis = [-force / beta]
        lap_basis = []
        jac_diag = 1.0 - 3.0 * field * field
        hess = jnp.zeros((ITERS + 1, ITERS), jnp.float32)
        for k in range(ITERS):
            lap_vec = laplace(basis[k])
            lap_basis.append(lap_vec)
            image = DIFFUSION * lap_vec + jac_diag * basis[k]
            heights_local = jnp.stack([jnp.sum(vec * image) for vec in basis])
            summed = lax.psum(heights_local, ("px", "py"))
            rest = image
            for j in range(k + 1):
                rest = rest - summed[j] * basis[j]
            height = jnp.sqrt(lax.psum(jnp.sum(rest * rest), ("px", "py")) + EPS)
            hess = hess.at[: k + 1, k].set(summed).at[k + 1, k].set(height)
            if k < ITERS - 1:
                basis.append(rest / height)
        coeffs = solve_small(hess, beta)
        delta = coeffs[0] * basis[0]
        for j in range(1, ITERS):
            delta = delta + coeffs[j] * basis[j]
        inner = lax.psum(jnp.sum(diffs * delta[None], axis=(1, 2, 3)), ("px", "py"))
        mean_dist = first_sum / cells + EPS
        weight = 1.0 / mean_dist + SHIFT
        total = jnp.sum(2.0 * inner / (cells * mean_dist * mean_dist * weight))
        scale = 1.0 / (1.0 + jnp.abs(total))
        field = field + scale * delta
        lap_field = laplace(field)
    return (field, allen_cahn(field, lap_field))


def solution(mesh):
    placed = (P("px", "py", None), P(None, "px", "py", None))
    return jax.shard_map(
        local,
        mesh=mesh,
        in_specs=placed,
        out_specs=(P("px", "py", None), P("px", "py", None)),
        check_vma=False,
    )
```

profile of v0, /device:TPU:38, one launch (start us, length us, event | category | flops | bytes accessed | tf_op | source)
XLA Modules:
  0.0 1435.6 jit_solution(6165251050151356504)
XLA Ops:
  1.5 2.7 collective-permute-start
  4.2 5.2 collective-permute-start.1
  19.9 80.0 %psum.126 = f32[]{:T(128)} all-reduce(f32[]{:T(128)} %get-tuple-element.179), channel_id=1, replica_groups=mesh['px'=16,'py'=16] {'px','py'}, use_global_device_ids=true, to_apply=%region_1.0 | all-reduce | flops 1 | bytes 8 | tf_op jit(solution)/shard_map/psum | solution.py:78
  100.6 3.4 collective-permute-start.5
  104.0 2.5 collective-permute-start.4
  107.2 4.7 collective-permute-done.4
  116.5 2.5 collective-permute-done.7
  119.8 73.3 %psum.127 = f32[1]{0:T(128)} all-reduce(f32[1]{0:T(128)} %bitcast), channel_id=1, replica_groups=mesh['px'=16,'py'=16] {'px','py'}, use_global_device_ids=true, to_apply=%region_3.0 | all-reduce | flops 1 | bytes 8 | tf_op jit(solution)/shard_map/psum | solution.py:89
  194.5 74.3 %psum.128 = f32[]{:T(128)} all-reduce(f32[]{:T(128)} %multiply_reduce_fusion.21), channel_id=1, replica_groups=mesh['px'=16,'py'=16] {'px','py'}, use_global_device_ids=true, to_apply=%region_5.0 | all-reduce | flops 1 | bytes 8 | tf_op jit(solution)/shard_map/psum | solution.py:93
  270.2 3.4 collective-permute-start.9
  273.6 2.5 collective-permute-start.8
  277.3 4.1 collective-permute-done.8
  291.0 73.4 %psum.129 = f32[2]{0:T(128)S(1)} all-reduce(f32[2]{0:T(128)S(1)} %pad_maximum_fusion.92), channel_id=1, replica_groups=mesh['px'=16,'py'=16] {'px','py'}, use_global_device_ids=true, to_apply=%region_9.0 | all-reduce | flops 2 | bytes 16 | tf_op jit(solution)/shard_map/psum | solution.py:89
  367.1 74.1 %psum.130 = f32[]{:T(128)} all-reduce(f32[]{:T(128)} %get-tuple-element.174), channel_id=1, replica_groups=mesh['px'=16,'py'=16] {'px','py'}, use_global_device_ids=true, to_apply=%region_11.0 | all-reduce | flops 1 | bytes 8 | tf_op jit(solution)/shard_map/psum | solution.py:93
  441.9 3.4 collective-permute-start.13
  448.6 4.6 collective-permute-done.12
  461.1 2.8 multiply_reduce_fusion.17
  466.0 75.2 %psum.131 = f32[3]{0:T(128)S(1)} all-reduce(f32[3]{0:T(128)S(1)} %pad_maximum_fusion.93), channel_id=1, replica_groups=mesh['px'=16,'py'=16] {'px','py'}, use_global_device_ids=true, to_apply=%region_16.0 | all-reduce | flops 3 | bytes 24 | tf_op jit(solution)/shard_map/psum | solution.py:89
  543.7 3.6 multiply_reduce_fusion.14
  548.8 74.0 %psum.132 = f32[]{:T(128)} all-reduce(f32[]{:T(128)} %multiply_reduce_fusion.14), channel_id=1, replica_groups=mesh['px'=16,'py'=16] {'px','py'}, use_global_device_ids=true, to_apply=%region_18.0 | all-reduce | flops 1 | bytes 8 | tf_op jit(solution)/shard_map/psum | solution.py:93
  636.7 73.7 %all-reduce.21 = (f32[8]{0:T(128)S(1)}, f32[8]{0:T(128)S(1)}) all-reduce(f32[8]{0:T(128)S(1)} %get-tuple-element.150, f32[8]{0:T(128)S(1)} %get-tuple-element.149), channel_id=1, replica_groups=mesh['px'=16,'py'=16] {'px','py'}, use_global_device_ids=true, to_apply=%region_25.27 | all-reduce | flops 16 | bytes 128 | tf_op jit(solution)/shard_map/psum | solution.py:78
  711.9 3.3 collective-permute-start.17
  715.2 2.5 collective-permute-start.16
  717.7 5.4 collective-permute-done.16
  727.6 2.5 collective-permute-done.19
  731.0 73.4 %psum.135 = f32[]{:T(128)} all-reduce(f32[]{:T(128)} %get-tuple-element.171), channel_id=1, replica_groups=mesh['px'=16,'py'=16] {'px','py'}, use_global_device_ids=true, to_apply=%region_28.0 | all-reduce | flops 1 | bytes 8 | tf_op jit(solution)/shard_map/psum | solution.py:78
  805.1 3.4 collective-permute-start.21
  808.5 2.5 collective-permute-start.20
  811.0 5.4 collective-permute-done.20
  820.9 2.5 collective-permute-done.23
  824.3 73.4 %psum.136 = f32[1]{0:T(128)} all-reduce(f32[1]{0:T(128)} %bitcast.32), channel_id=1, replica_groups=mesh['px'=16,'py'=16] {'px','py'}, use_global_device_ids=true, to_apply=%region_30.0 | all-reduce | flops 1 | bytes 8 | tf_op jit(solution)/shard_map/psum | solution.py:89
  899.0 74.1 %psum.137 = f32[]{:T(128)} all-reduce(f32[]{:T(128)} %multiply_reduce_fusion.11), channel_id=1, replica_groups=mesh['px'=16,'py'=16] {'px','py'}, use_global_device_ids=true, to_apply=%region_32.0 | all-reduce | flops 1 | bytes 8 | tf_op jit(solution)/shard_map/psum | solution.py:93
  974.5 3.4 collective-permute-start.25
  977.9 2.5 collective-permute-start.24
  980.4 5.4 collective-permute-done.24
  995.3 73.4 %psum.138 = f32[2]{0:T(128)S(1)} all-reduce(f32[2]{0:T(128)S(1)} %pad_maximum_fusion.94), channel_id=1, replica_groups=mesh['px'=16,'py'=16] {'px','py'}, use_global_device_ids=true, to_apply=%region_35.0 | all-reduce | flops 2 | bytes 16 | tf_op jit(solution)/shard_map/psum | solution.py:89
  1071.4 74.0 %psum.139 = f32[]{:T(128)} all-reduce(f32[]{:T(128)} %get-tuple-element.166), channel_id=1, replica_groups=mesh['px'=16,'py'=16] {'px','py'}, use_global_device_ids=true, to_apply=%region_37.0 | all-reduce | flops 1 | bytes 8 | tf_op jit(solution)/shard_map/psum | solution.py:93
  1146.1 3.4 collective-permute-start.29
  1152.9 4.6 collective-permute-done.28
  1166.0 2.7 multiply_reduce_fusion.7
  1170.8 75.2 %psum.140 = f32[3]{0:T(128)S(1)} all-reduce(f32[3]{0:T(128)S(1)} %pad_maximum_fusion.95), channel_id=1, replica_groups=mesh['px'=16,'py'=16] {'px','py'}, use_global_device_ids=true, to_apply=%region_41.0 | all-reduce | flops 3 | bytes 24 | tf_op jit(solution)/shard_map/psum | solution.py:89
  1248.5 3.6 multiply_reduce_fusion.4
  1253.5 74.1 %psum.141 = f32[]{:T(128)} all-reduce(f32[]{:T(128)} %multiply_reduce_fusion.4), channel_id=1, replica_groups=mesh['px'=16,'py'=16] {'px','py'}, use_global_device_ids=true, to_apply=%region_43.0 | all-reduce | flops 1 | bytes 8 | tf_op jit(solution)/shard_map/psum | solution.py:93
  1341.6 73.5 %all-reduce.20 = (f32[8]{0:T(128)S(1)}, f32[8]{0:T(128)S(1)}) all-reduce(f32[8]{0:T(128)S(1)} %get-tuple-element.148, f32[8]{0:T(128)S(1)} %get-tuple-element.147), channel_id=1, replica_groups=mesh['px'=16,'py'=16] {'px','py'}, use_global_device_ids=true, to_apply=%region_48.0 | all-reduce | flops 16 | bytes 128 | tf_op jit(solution)/shard_map/psum | solution.py:78
  1416.4 3.3 collective-permute-start.33
  1419.8 2.5 collective-permute-start.32
  1422.3 5.4 collective-permute-done.32
  1432.2 2.5 collective-permute-done.35
  (157 shorter events, 107.0 us)
Async XLA Ops:
  0.6 18.4 %copy-start = (f32[8,16,512]{2,1,0:T(8,128)S(1)}, f32[8,16,512]{2,1,0:T(8,128)}, u32[]{:S(2)}) copy-start(f32[8,16,512]{2,1,0:T(8,128)} %param.27) | copy-start | bytes 786436
  1.5 10.5 collective-permute-start
  4.2 6.8 collective-permute-start.1
  12.0 5.6 collective-permute-start.2
  14.0 5.1 collective-permute-start.3
  100.6 6.5 collective-permute-start.5
  104.0 7.9 collective-permute-start.4
  112.0 4.5 collective-permute-start.6
  113.9 5.1 collective-permute-start.7
  270.2 7.1 collective-permute-start.9
  273.6 7.9 collective-permute-start.8
  281.5 5.1 collective-permute-start.10
  283.4 5.1 collective-permute-start.11
  441.9 6.7 collective-permute-start.13
  445.3 7.9 collective-permute-start.12
  453.2 7.9 collective-permute-start.14
  455.1 6.0 collective-permute-start.15
  461.1 175.0 %copy-start.1 = (f32[8,8,16,512]{3,2,1,0:T(8,128)S(1)}, f32[8,8,16,512]{3,2,1,0:T(8,128)}, u32[]{:S(2)}) copy-start(f32[8,8,16,512]{3,2,1,0:T(8,128)} %param.28) | copy-start | bytes 6291460
  711.9 5.9 collective-permute-start.17
  715.2 7.9 collective-permute-start.16
  723.1 4.5 collective-permute-start.18
  725.0 5.1 collective-permute-start.19
  805.1 5.9 collective-permute-start.21
  808.5 7.9 collective-permute-start.20
  816.4 4.5 collective-permute-start.22
  818.3 5.1 collective-permute-start.23
  974.5 5.9 collective-permute-start.25
  977.9 7.9 collective-permute-start.24
  985.8 5.1 collective-permute-start.26
  987.8 5.1 collective-permute-start.27
  1146.1 6.7 collective-permute-start.29
  1149.5 7.9 collective-permute-start.28
  1158.1 7.9 collective-permute-start.30
  1160.0 6.0 collective-permute-start.31
  1416.4 19.2 %copy-start.2 = (f32[8,16,512]{2,1,0:T(8,128)}, f32[8,16,512]{2,1,0:T(8,128)S(1)}, u32[]{:S(2)}) copy-start(f32[8,16,512]{2,1,0:T(8,128)S(1)} %multiply_add_fusion) | copy-start | bytes 786436
  1416.4 5.9 collective-permute-start.33
  1419.8 7.9 collective-permute-start.32
  1427.7 4.5 collective-permute-start.34
  1429.6 5.1 collective-permute-start.35
where the time goes:
time: 1440 us
  blocking collectives  1190 us (83%)
  starting transfers between devices  93.6 us (6%)
  waiting for transfers between devices  55.3 us (4%)
  other arithmetic  50.1 us (3%)
  between operations  27.2 us (2%)
  local copies, waits for them, and re-layouts  20.1 us (1%)
    psum x6, blocking collectives, local(): height = jnp.sqrt(lax.psum(jnp.sum(rest * rest), ('px', 'py')) + EPS)  445 us
    psum x6, blocking collectives, local(): summed = lax.psum(heights_local, ('px', 'py'))  444 us
    psum x4, blocking collectives, local(): lax.psum((dist_local, jnp.sum(force * force)), ('px', 'py'))  301 us
    ppermute x18, starting transfers between devices, extended(): lax.ppermute(tail, axis, [(i, (i + 1) % count) for i in range(ends)])  53.6 us
    ppermute x18, starting transfers between devices, extended(): lax.ppermute(head, axis, [((i + 1) % count, i) for i in range(ends)])  40 us
    ppermute x18, waiting for transfers between devices, extended(): lax.ppermute(head, axis, [((i + 1) % count, i) for i in range(ends)])  39.6 us
  transfers between devices with their start and end apart: 36, of which 16 were waited for; matrix products, arithmetic and copies ran while one was open for 1% of the time, Pallas kernels for 0%

commit v1 on v0

--- a/solution.py
+++ b/solution.py
@@ -86,7 +86,7 @@
             lap_basis.append(lap_vec)
             image = DIFFUSION * lap_vec + jac_diag * basis[k]
             heights_local = jnp.stack([jnp.sum(vec * image) for vec in basis])
-            summed = lax.psum(heights_local, ("px", "py"))
+            summed = jnp.sum(lax.all_gather(heights_local, ("px", "py")), axis=0)
             rest = image
             for j in range(k + 1):
                 rest = rest - summed[j] * basis[j]

time: 1440 us -> 1440 us (level)
  waiting for transfers between devices: 55.3 us -> 26.5 us
  starting transfers between devices: 93.6 us -> 108 us
    unnamed x0 -> x6, blocking collectives: none -> 453 us
    psum x6 -> x0, blocking collectives: 444 us -> none  [local(): summed = lax.psum(heights_local, ('px', 'py'))]
    ppermute x18, waiting for transfers between devices: 39.6 us -> 3.31 us  [extended(): lax.ppermute(head, axis, [((i + 1) % count, i) for i in range(ends)])]
    ppermute x18, starting transfers between devices: 53.6 us -> 71.7 us  [extended(): lax.ppermute(tail, axis, [(i, (i + 1) % count) for i in range(ends)])]
where the time goes in v1:
time: 1440 us
  blocking collectives  1200 us (83%)
  starting transfers between devices  108 us (8%)
  other arithmetic  53.1 us (4%)
  between operations  27.5 us (2%)
  waiting for transfers between devices  26.5 us (2%)
  local copies, waits for them, and re-layouts  22.8 us (2%)
    unnamed x6, blocking collectives  453 us
    psum x6, blocking collectives, local(): height = jnp.sqrt(lax.psum(jnp.sum(rest * rest), ('px', 'py')) + EPS)  446 us
    psum x4, blocking collectives, local(): lax.psum((dist_local, jnp.sum(force * force)), ('px', 'py'))  299 us
    ppermute x18, starting transfers between devices, extended(): lax.ppermute(tail, axis, [(i, (i + 1) % count) for i in range(ends)])  71.7 us
    ppermute x18, starting transfers between devices, extended(): lax.ppermute(head, axis, [((i + 1) % count, i) for i in range(ends)])  36.7 us
  transfers between devices with their start and end apart: 36, of which 16 were waited for; matrix products, arithmetic and copies ran while one was open for 1% of the time, Pallas kernels for 0%

profile of v1, /device:TPU:38, one launch (start us, length us, event | category | flops | bytes accessed | tf_op | source)
XLA Modules:
  0.0 1436.0 jit_solution(16213385688685286768)
XLA Ops:
  1.5 3.4 collective-permute-start.1
  4.9 2.4 collective-permute-start
  9.5 3.3 collective-permute-done
  14.8 2.4 collective-permute-start.3
  20.7 76.8 %psum.84 = f32[]{:T(128)} all-reduce(f32[]{:T(128)} %get-tuple-element.179), channel_id=1, replica_groups=mesh['px'=16,'py'=16] {'px','py'}, use_global_device_ids=true, to_apply=%region_1.0 | all-reduce | flops 1 | bytes 8 | tf_op jit(solution)/shard_map/psum | solution.py:78
  98.2 2.5 collective-permute-start.4
  100.7 5.4 collective-permute-start.5
  109.7 2.4 collective-permute-start.7
  112.3 2.5 collective-permute-done.7
  116.4 74.7 %all-reduce.20 = f32[256]{0:T(256)S(1)} all-reduce(f32[256]{0:T(256)S(1)} %dynamic-update-slice.26), channel_id=1, replica_groups=mesh['px'=16,'py'=16] {'px','py'}, use_global_device_ids=true, to_apply=%add.20 | all-reduce | flops 256 | bytes 2048
  193.0 74.3 %psum.85 = f32[]{:T(128)} all-reduce(f32[]{:T(128)} %multiply_reduce_fusion.21), channel_id=1, replica_groups=mesh['px'=16,'py'=16] {'px','py'}, use_global_device_ids=true, to_apply=%region_5.0 | all-reduce | flops 1 | bytes 8 | tf_op jit(solution)/shard_map/psum | solution.py:93
  270.6 6.0 collective-permute-start.9
  280.2 2.4 collective-permute-start.11
  287.6 74.7 %all-reduce.21 = f32[512]{0:T(512)S(1)} all-reduce(f32[512]{0:T(512)S(1)} %maximum_dynamic-update-slice_fusion), channel_id=2, replica_groups=mesh['px'=16,'py'=16] {'px','py'}, use_global_device_ids=true, to_apply=%add.21 | all-reduce | flops 512 | bytes 4096
  363.0 2.1 multiply_reduce_fusion.18
  365.1 74.5 %psum.86 = f32[]{:T(128)} all-reduce(f32[]{:T(128)} %get-tuple-element.174), channel_id=1, replica_groups=mesh['px'=16,'py'=16] {'px','py'}, use_global_device_ids=true, to_apply=%region_11.0 | all-reduce | flops 1 | bytes 8 | tf_op jit(solution)/shard_map/psum | solution.py:93
  442.3 6.0 collective-permute-start.13
  451.9 2.4 collective-permute-start.15
  457.9 2.8 multiply_reduce_fusion.17
  462.8 76.4 %all-reduce.22 = f32[768]{0:T(1024)S(1)} all-reduce(f32[768]{0:T(1024)S(1)} %maximum_dynamic-update-slice_fusion.1), channel_id=3, replica_groups=mesh['px'=16,'py'=16] {'px','py'}, use_global_device_ids=true, to_apply=%add.22 | all-reduce | flops 768 | bytes 6144
  540.0 3.6 multiply_reduce_fusion.14
  543.7 74.4 %psum.87 = f32[]{:T(128)} all-reduce(f32[]{:T(128)} %multiply_reduce_fusion.14), channel_id=1, replica_groups=mesh['px'=16,'py'=16] {'px','py'}, use_global_device_ids=true, to_apply=%region_18.0 | all-reduce | flops 1 | bytes 8 | tf_op jit(solution)/shard_map/psum | solution.py:93
  635.6 73.4 %all-reduce.27 = (f32[8]{0:T(128)S(1)}, f32[8]{0:T(128)S(1)}) all-reduce(f32[8]{0:T(128)S(1)} %get-tuple-element.150, f32[8]{0:T(128)S(1)} %get-tuple-element.149), channel_id=1, replica_groups=mesh['px'=16,'py'=16] {'px','py'}, use_global_device_ids=true, to_apply=%region_25.27 | all-reduce | flops 16 | bytes 128 | tf_op jit(solution)/shard_map/psum | solution.py:78
  712.3 6.0 collective-permute-start.17
  721.9 2.4 collective-permute-start.19
  724.4 2.5 collective-permute-done.19
  727.8 74.5 %psum.90 = f32[]{:T(128)} all-reduce(f32[]{:T(128)} %get-tuple-element.171), channel_id=1, replica_groups=mesh['px'=16,'py'=16] {'px','py'}, use_global_device_ids=true, to_apply=%region_28.0 | all-reduce | flops 1 | bytes 8 | tf_op jit(solution)/shard_map/psum | solution.py:78
  803.0 3.0 collective-permute-start.20
  805.9 5.0 collective-permute-start.21
  814.5 2.4 collective-permute-start.23
  817.1 2.5 collective-permute-done.23
  821.2 75.8 %all-reduce.23 = f32[256]{0:T(256)S(1)} all-reduce(f32[256]{0:T(256)S(1)} %dynamic-update-slice.29), channel_id=1, replica_groups=mesh['px'=16,'py'=16] {'px','py'}, use_global_device_ids=true, to_apply=%add.23 | all-reduce | flops 256 | bytes 2048
  898.9 74.2 %psum.91 = f32[]{:T(128)} all-reduce(f32[]{:T(128)} %multiply_reduce_fusion.11), channel_id=1, replica_groups=mesh['px'=16,'py'=16] {'px','py'}, use_global_device_ids=true, to_apply=%region_32.0 | all-reduce | flops 1 | bytes 8 | tf_op jit(solution)/shard_map/psum | solution.py:93
  976.5 6.0 collective-permute-start.25
  986.1 2.4 collective-permute-start.27
  994.6 75.3 %all-reduce.24 = f32[512]{0:T(512)S(1)} all-reduce(f32[512]{0:T(512)S(1)} %maximum_dynamic-update-slice_fusion.2), channel_id=4, replica_groups=mesh['px'=16,'py'=16] {'px','py'}, use_global_device_ids=true, to_apply=%add.24 | all-reduce | flops 512 | bytes 4096
  1072.7 74.5 %psum.92 = f32[]{:T(128)} all-reduce(f32[]{:T(128)} %get-tuple-element.166), channel_id=1, replica_groups=mesh['px'=16,'py'=16] {'px','py'}, use_global_device_ids=true, to_apply=%region_37.0 | all-reduce | flops 1 | bytes 8 | tf_op jit(solution)/shard_map/psum | solution.py:93
  1149.8 6.0 collective-permute-start.29
  1160.0 2.4 collective-permute-start.31
  1166.0 2.7 multiply_reduce_fusion.7
  1168.7 2.1 maximum_dynamic-update-slice_fusion.3
  1170.8 76.4 %all-reduce.25 = f32[768]{0:T(1024)S(1)} all-reduce(f32[768]{0:T(1024)S(1)} %maximum_dynamic-update-slice_fusion.3), channel_id=5, replica_groups=mesh['px'=16,'py'=16] {'px','py'}, use_global_device_ids=true, to_apply=%add.25 | all-reduce | flops 768 | bytes 6144
  1248.1 3.7 multiply_reduce_fusion.4
  1251.9 73.7 %psum.93 = f32[]{:T(128)} all-reduce(f32[]{:T(128)} %multiply_reduce_fusion.4), channel_id=1, replica_groups=mesh['px'=16,'py'=16] {'px','py'}, use_global_device_ids=true, to_apply=%region_43.0 | all-reduce | flops 1 | bytes 8 | tf_op jit(solution)/shard_map/psum | solution.py:93
  1342.9 74.2 %all-reduce.26 = (f32[8]{0:T(128)S(1)}, f32[8]{0:T(128)S(1)}) all-reduce(f32[8]{0:T(128)S(1)} %get-tuple-element.148, f32[8]{0:T(128)S(1)} %get-tuple-element.147), channel_id=1, replica_groups=mesh['px'=16,'py'=16] {'px','py'}, use_global_device_ids=true, to_apply=%region_48.0 | all-reduce | flops 16 | bytes 128 | tf_op jit(solution)/shard_map/psum | solution.py:78
  1420.4 6.0 collective-permute-start.33
  1430.0 2.4 collective-permute-start.35
  1432.5 2.5 collective-permute-done.35
  (175 shorter events, 100.9 us)
Async XLA Ops:
  0.6 19.2 %copy-start = (f32[8,16,512]{2,1,0:T(8,128)S(1)}, f32[8,16,512]{2,1,0:T(8,128)}, u32[]{:S(2)}) copy-start(f32[8,16,512]{2,1,0:T(8,128)} %param.27) | copy-start | bytes 786436
  1.5 7.1 collective-permute-start.1
  4.9 7.9 collective-permute-start
  12.8 5.7 collective-permute-start.2
  14.8 5.1 collective-permute-start.3
  98.2 8.6 collective-permute-start.4
  100.7 7.0 collective-permute-start.5
  107.8 4.5 collective-permute-start.6
  109.7 5.1 collective-permute-start.7
  268.7 9.2 collective-permute-start.8
  270.6 7.6 collective-permute-start.9
  278.2 5.3 collective-permute-start.10
  280.2 5.1 collective-permute-start.11
  440.4 8.8 collective-permute-start.12
  442.3 7.6 collective-permute-start.13
  450.0 7.9 collective-permute-start.14
  451.9 6.0 collective-permute-start.15
  457.9 177.2 %copy-start.1 = (f32[8,8,16,512]{3,2,1,0:T(8,128)S(1)}, f32[8,8,16,512]{3,2,1,0:T(8,128)}, u32[]{:S(2)}) copy-start(f32[8,8,16,512]{3,2,1,0:T(8,128)} %param.28) | copy-start | bytes 6291460
  710.4 8.0 collective-permute-start.16
  712.3 7.6 collective-permute-start.17
  719.9 4.5 collective-permute-start.18
  721.9 5.1 collective-permute-start.19
  803.0 8.0 collective-permute-start.20
  805.9 6.6 collective-permute-start.21
  812.6 4.5 collective-permute-start.22
  814.5 5.1 collective-permute-start.23
  974.6 8.0 collective-permute-start.24
  976.5 7.6 collective-permute-start.25
  984.1 5.9 collective-permute-start.26
  986.1 5.1 collective-permute-start.27
  1147.9 8.8 collective-permute-start.28
  1149.8 7.6 collective-permute-start.29
  1158.1 7.9 collective-permute-start.30
  1160.0 6.0 collective-permute-start.31
  1418.4 17.5 %copy-start.2 = (f32[8,16,512]{2,1,0:T(8,128)}, f32[8,16,512]{2,1,0:T(8,128)S(1)}, u32[]{:S(2)}) copy-start(f32[8,16,512]{2,1,0:T(8,128)S(1)} %multiply_add_fusion) | copy-start | bytes 786436
  1418.5 8.0 collective-permute-start.32
  1420.4 7.6 collective-permute-start.33
  1428.0 4.5 collective-permute-start.34
  1430.0 5.1 collective-permute-start.35
